TPU v7x, 128 devices: a whole 4x4x4 slice. The times are simulated.
128 devices in a mesh: row: 8 (over y, core), col: 16 (over x, z).
Axes of the slice: x: 4, y: 4, z: 4, core: 2. Of those that a mesh axis runs over, the one named last changes fastest.
Arguments:
- tokens: bfloat16 [1024, 8192], P('row', 'col'), may hold values from -6 to 6
- gate_weight: bfloat16 [8192, 28672], P('col', 'row'), may hold values from -0.09375 to 0.09375
- up_weight: bfloat16 [8192, 28672], P('col', 'row'), may hold values from -0.09375 to 0.09375
- down_weight: bfloat16 [28672, 8192], P('row', 'col'), may hold values from -0.046875 to 0.046875
- gate_mask: int32 [64, 224], P('col', 'row'), may hold values 0 or 1
- up_mask: int32 [64, 224], P('col', 'row'), may hold values 0 or 1
- down_mask: int32 [224, 64], P('row', 'col'), may hold values 0 or 1
Outputs:
- mixed_out: bfloat16 [1024, 8192], P('row', 'col')
Inputs may be any that keep to these rules, and one draw needn't show every extreme that they name: `gate_mask`: each entry keeps (1) or drops (0) one block. `up_mask`: each entry keeps (1) or drops (0) one block. `down_mask`: each entry keeps (1) or drops (0) one block.
All inputs are finite; a program needn't handle non-finite values.
Results may differ from a plain program's by a relative error of at most 0.025.
Values may be sent and summed in bfloat16 or wider, within the bound.
A program may use at most 128 MiB of HBM per device.

v0:
```python
import jax
import jax.numpy as jnp
from jax import lax
from jax.sharding import PartitionSpec as P


def expand(weight, block_mask):
    row_count, col_count = weight.shape
    mask_rows, mask_cols = block_mask.shape
    shaped = weight.reshape(mask_rows, row_count // mask_rows, mask_cols, col_count // mask_cols)
    kept_blocks = shaped * block_mask.astype(weight.dtype)[:, None, :, None]
    return kept_blocks.reshape(row_count, col_count)


def per_device(tokens, gate_weight, up_weight, down_weight, gate_mask, up_mask, down_mask):
    kept_gate = expand(gate_weight, gate_mask)
    kept_up = expand(up_weight, up_mask)
    kept_down = expand(down_weight, down_mask)
    gathered = lax.all_gather(tokens, "row", axis=0, tiled=True)
    gate_part = jnp.dot(gathered, kept_gate, preferred_element_type=jnp.float32)
    up_part = jnp.dot(gathered, kept_up, preferred_element_type=jnp.float32)
    gate_sum, up_sum = (
        lax.psum(gate_part.astype(jnp.bfloat16), "col").astype(jnp.float32),
        lax.psum(up_part.astype(jnp.bfloat16), "col").astype(jnp.float32),
    )
    hidden = (jax.nn.silu(gate_sum) * up_sum).astype(jnp.bfloat16)
    return lax.psum_scatter(
        jnp.dot(hidden, kept_down, preferred_element_type=jnp.float32).astype(jnp.bfloat16),
        "row",
        scatter_dimension=0,
        tiled=True,
    )


def solution(mesh):
    return jax.shard_map(
        per_device,
        mesh=mesh,
        in_specs=(
            P("row", "col"),
            P("col", "row"),
            P("col", "row"),
            P("row", "col"),
            P("col", "row"),
            P("col", "row"),
            P("row", "col"),
        ),
        out_specs=P("row", "col"),
        check_vma=False,
    )
```

profile of v0, /device:TPU:0, one launch (start us, length us, event | category | flops | bytes accessed | tf_op | source)
XLA Modules:
  0.0 304.0 jit_solution(16321837674155461157)
XLA Ops:
  6.5 0.0 all-gather.2.cloned.1.call-start
  6.5 0.7 all-gather.2.cloned.1.call-update
  7.3 0.0 all-reduce.3.cloned.1.call-start
  7.3 0.7 convert_element_type.33
  8.0 0.1 copy.9
  8.1 0.0 copy-start.2
  8.1 6.0 %copy.10 = bf16[512,3584]{0,1:T(8,128)(2,1)} copy(bf16[512,3584]{1,0:T(8,128)(2,1)} %param.8) | data formatting | bytes 7340032 | tf_op args[1]
  14.1 0.0 copy-done.2
  14.1 0.1 copy.11
  14.2 5.9 %copy.12 = bf16[512,3584]{0,1:T(8,128)(2,1)} copy(bf16[512,3584]{1,0:T(8,128)(2,1)} %param.9) | data formatting | bytes 7340032 | tf_op args[2]
  20.1 14.7 %all-gather.2.cloned.1.call-done = bf16[1024,512]{1,0:T(8,128)(2,1)} async-done(((bf16[128,512]{1,0:T(8,128)(2,1)}), bf16[1024,512]{1,0:T(8,128)(2,1)}) %all-gather.2.cloned.1.call-update) | async-done | bytes 1048592 | tf_op jit(solution)/shard_map/all_gather | solution.py:19
  34.8 0.0 copy-start.1
  34.8 1.0 mul.40
  35.8 1.0 copy-done.1
  36.9 0.0 copy-start.5
  36.9 7.4 %fusion.7 = bf16[1024,3584]{0,1:T(8,128)(2,1)} fusion(bf16[1024,512]{1,0:T(8,128)(2,1)} %all-gather.2.cloned.1.call-done, bf16[512,3584]{0,1:T(8,128)(2,1)S(1)} %copy-done.1, bf16[448,8,4,128]{3,2,1,0:T(4,128)(2,1)S(1)} %bitcast.29), kind=kOutput, calls=%fused_computation.10 | convolution fusion | flops 3763601408 | bytes 15728640 | tf_op jit(solution)/shard_map/dot_general | solution.py:20
  44.3 0.0 copy-start
  44.3 1.0 mul.44
  45.3 0.0 copy-done.5
  45.3 1.0 copy-done
  46.4 6.1 %fusion.8 = bf16[1024,3584]{0,1:T(8,128)(2,1)} fusion(bf16[1024,512]{1,0:T(8,128)(2,1)S(1)} %copy-done.5, bf16[512,3584]{0,1:T(8,128)(2,1)S(1)} %copy-done, bf16[448,8,4,128]{3,2,1,0:T(4,128)(2,1)S(1)} %bitcast.27), kind=kOutput, calls=%fused_computation.11 | convolution fusion | flops 3763601408 | bytes 15728640 | tf_op jit(solution)/shard_map/dot_general | solution.py:21
  52.4 0.0 copy-start.3
  52.4 0.0 all-reduce.3.cloned.1.call-update
  52.5 0.0 reduce-scatter.2.cloned.1.call-start
  52.5 0.6 copy-done.3
  53.1 0.1 copy.13
  53.2 198.4 %all-reduce.3.cloned.1.call-done = (bf16[1024,3584]{0,1:T(8,128)(2,1)}, bf16[1024,3584]{0,1:T(8,128)(2,1)}) async-done(((bf16[1024,3584]{0,1:T(8,128)(2,1)}, bf16[1024,3584]{0,1:T(8,128)(2,1)}), (bf16[1024,3584]{0,1:T(8,128)(2,1)}, bf16[1024,3584]{0,1:T(8,128)(2,1)})) %all-reduce.3.cloned.1.call-update) | async-done | bytes 14680080 | tf_op jit(solution)/shard_map/psum | solution.py:24
  251.6 0.0 copy-start.4
  251.6 1.0 mul.48
  252.7 1.0 copy-done.4
  253.7 11.6 %fusion.12 = bf16[1024,512]{1,0:T(8,128)(2,1)} fusion(bf16[3584,512]{1,0:T(8,128)(2,1)S(1)} %copy-done.4, bf16[448,8,4,128]{3,2,1,0:T(4,128)(2,1)S(1)} %bitcast.28, bf16[1024,3584]{0,1:T(8,128)(2,1)} %get-tuple-element.5, bf16[1024,3584]{0,1:T(8,128)(2,1)} %get-tuple-element.6), kind=kOutput, calls=%fused_computation.18 | convolution fusion | flops 3789815808 | bytes 23068672 | tf_op jit(solution)/shard_map/dot_general | solution.py:28
  265.3 0.0 reduce-scatter.2.cloned.1.call-update
  265.3 32.1 %reduce-scatter.2.cloned.1.call-done = bf16[128,512]{1,0:T(8,128)(2,1)} async-done(((bf16[1024,512]{1,0:T(8,128)(2,1)}), bf16[128,512]{1,0:T(8,128)(2,1)}) %reduce-scatter.2.cloned.1.call-update) | async-done | bytes 131088 | tf_op jit(solution)/shard_map/reduce_scatter | solution.py:27
  (2 shorter events, 0.0 us)
Async XLA Ops:
  6.5 28.3 %all-gather.2.cloned.1.call-start = ((), (), s32[]{:S(2)}) async-start(), calls=%async_computation.1 | async-start | bytes 1179648 | tf_op jit(solution)/shard_map/all_gather | solution.py:19
  7.3 244.4 %all-reduce.3.cloned.1.call-start = ((), (), s32[]{:S(2)}) async-start(), calls=%async_computation.3 | async-start | bytes 29360128 | tf_op jit(solution)/shard_map/psum | solution.py:24
  8.1 6.0 %copy-start.2 = (s32[4,28]{1,0:T(4,128)S(1)}, s32[4,28]{1,0:T(4,128)}, u32[]{:S(2)}) copy-start(s32[4,28]{1,0:T(4,128)} %param.12) | copy-start | bytes 1348
  34.8 2.0 copy-start.1
  36.9 8.5 %copy-start.5 = (bf16[1024,512]{1,0:T(8,128)(2,1)S(1)}, bf16[1024,512]{1,0:T(8,128)(2,1)}, u32[]{:S(2)}) copy-start(bf16[1024,512]{1,0:T(8,128)(2,1)} %all-gather.2.cloned.1.call-done) | copy-start | bytes 3145732
  44.3 2.0 copy-start
  52.4 0.7 copy-start.3
  52.5 245.0 %reduce-scatter.2.cloned.1.call-start = ((), (), s32[]{:S(2)}) async-start(), calls=%async_computation.2 | async-start | bytes 1179648 | tf_op jit(solution)/shard_map/reduce_scatter | solution.py:27
  251.6 2.0 copy-start.4
Sparse Core Ops, SparseCore 0:
  9.0 25.7 all-gather.1
  52.6 199.0 all-reduce.2
  265.4 31.9 reduce-scatter.1
where the time goes:
time: 304 us
  waiting for transfers between devices  246 us (81%)
  matrix products  25.1 us (8%)
  local copies, waits for them, and re-layouts  18.9 us (6%)
  between operations  13.1 us (4%)
    psum x1, waiting for transfers between devices, per_device(): lax.psum(up_part.astype(jnp.bfloat16), 'col').astype(jnp.float32)  198 us
    reduce_scatter x1, waiting for transfers between devices, per_device(): lax.psum_scatter(jnp.dot(hidden, kept_down, preferred_element_type=jnp.fl...  32.1 us
    unnamed x14, local copies, waits for them, and re-layouts  15.6 us
    all_gather x1, waiting for transfers between devices, per_device(): gathered = lax.all_gather(tokens, 'row', axis=0, tiled=True)  14.7 us
    dot_general x1, matrix products, per_device(): jnp.dot(hidden, kept_down, preferred_element_type=jnp.float32)  11.6 us
    dot_general x1, matrix products, per_device(): gate_part = jnp.dot(gathered, kept_gate, preferred_element_type=jnp.float32)  7.45 us
    dot_general x1, matrix products, per_device(): up_part = jnp.dot(gathered, kept_up, preferred_element_type=jnp.float32)  6.08 us
  transfers between devices with their start and end apart: 3, of which 3 were waited for; matrix products, arithmetic and copies ran while one was open for 4% of the time, Pallas kernels for 0%

commit v1 on v0

v1 whole, which is shorter than its diff:
```python
import functools

import jax
import jax.numpy as jnp
from jax import lax
from jax.experimental import pallas as pl
from jax.experimental.pallas import tpu as pltpu
from jax.sharding import PartitionSpec as P

ROUNDS = 14
BLOCK = 128
LAGS = 8
F32, BF16 = jnp.float32, jnp.bfloat16
MESH = pl.DeviceIdType.MESH


def layer_kernel(
    tok_hbm, gate_hbm, up_hbm, down_hbm, gm, um, dm, out_ref,
    tok, w_gate, w_up, w_down,
    s1, r1h, r1f, part, s2, r2h, r2f, hid, acc, o_send, o_recv, oy_send, oy_h, oy_f,
    load_sem, tok_ss, tok_rs, rs_ss, rs_rs, ag_ss, ag_rs, out_ss, out_rs,
):
    cw = w_gate.shape[2]
    half_cw = cw // 2
    row, col = lax.axis_index("row"), lax.axis_index("col")
    y, core = row // 2, row % 2
    x, z = col // 4, col % 4
    coord = (x, z)

    def turn(v, k):
        return (v + k + 4) % 4

    def in_plane(axis, k):
        if axis == 0:
            return (row, turn(x, k) * 4 + z)
        return (row, x * 4 + turn(z, k))

    def in_line(k):
        return (turn(y, k) * 2 + core, col)

    twin = (row + 1 - 2 * core, col)
    step = (1, -1)

    def remote(src, dst, ss, rs, device):
        return pltpu.make_async_remote_copy(
            src_ref=src, dst_ref=dst, send_sem=ss, recv_sem=rs, device_id=device, device_id_type=MESH
        )

    def load_gate(j):
        return pltpu.make_async_copy(gate_hbm.at[:, pl.ds(pl.multiple_of(j * cw, cw), cw)], w_gate.at[j], load_sem.at[0, j])

    def load_up(j):
        return pltpu.make_async_copy(up_hbm.at[:, pl.ds(pl.multiple_of(j * cw, cw), cw)], w_up.at[j], load_sem.at[1, j])

    def load_down(j):
        return pltpu.make_async_copy(down_hbm.at[pl.ds(pl.multiple_of(j * cw, cw), cw)], w_down.at[j], load_sem.at[2, j])

    load_tok = pltpu.make_async_copy(tok_hbm, tok.at[y, pl.ds(2 * core, 2)], load_sem.at[3, 0])
    load_tok.start()

    @pl.loop(0, ROUNDS)
    def _(j):
        load_gate(j).start()
        load_up(j).start()

    @pl.loop(0, ROUNDS)
    def _(j):
        load_down(j).start()

    barrier = pltpu.get_barrier_semaphore()
    peers = [in_plane(a, k) for a in (0, 1) for k in step] + [in_line(k) for k in step] + [twin]
    for peer in peers:
        pl.semaphore_signal(barrier, inc=1, device_id=peer, device_id_type=MESH)
    pl.semaphore_wait(barrier, len(peers))

    mine = pl.ds(2 * core, 2)

    def tok_full(d):
        return remote(tok_hbm, tok.at[y, mine], tok_ss.at[d], tok_rs.at[d], in_line(step[d]))

    def tok_half(d):
        piece = tok.at[turn(y, -step[d]), 2 * core + d]
        return remote(piece, piece, tok_ss.at[2 + d], tok_rs.at[2 + d], in_line(step[d]))

    def tok_twin(k):
        piece = tok.at[turn(y, k), mine]
        return remote(piece, piece, tok_ss.at[4 + k % 4], tok_rs.at[4 + k % 4], twin)

    tok_full(0).start()
    tok_full(1).start()
    load_tok.wait()
    tok_twin(0).start()
    for d in (0, 1):
        tok_full(d).wait_recv()
        tok_half(d).start()
        tok_twin(-step[d]).start()
    for d in (0, 1):
        tok_half(d).wait_recv()
    tok_twin(2).start()
    for k in range(4):
        tok_twin(k).wait_recv()

    def rs1h(j, m, d):
        return remote(s1.at[j, m, 0, pl.ds(2 * d, 2)], r1h.at[j, m, d], rs_ss.at[m * 8 + d, j], rs_rs.at[m * 8 + d, j], in_plane(m, step[d]))

    def rs1f(j, m, d):
        k = m * 8 + 2 + d
        return remote(s1.at[j, m, 1 + d], r1f.at[j, m, d], rs_ss.at[k, j], rs_rs.at[k, j], in_plane(m, step[d]))

    def rs2h(j, m, d):
        k = m * 8 + 4 + d
        return remote(s2.at[j, m, 0, pl.ds(32 * d, 32)], r2h.at[j, m, d], rs_ss.at[k, j], rs_rs.at[k, j], in_plane(1 - m, step[d]))

    def rs2f(j, m, d):
        k = m * 8 + 6 + d
        return remote(s2.at[j, m, 1 + d], r2f.at[j, m, d], rs_ss.at[k, j], rs_rs.at[k, j], in_plane(1 - m, step[d]))

    def ag1f(j, t, d):
        k = t * 8 + d
        piece = hid.at[j, t, x, z]
        return remote(piece, piece, ag_ss.at[k, j], ag_rs.at[k, j], in_plane(t, step[d]))

    def ag1h(j, t, d):
        k = t * 8 + 2 + d
        half = pl.ds(32 * d, 32)
        piece = hid.at[j, 0, turn(x, -step[d]), z, half] if t == 0 else hid.at[j, 1, x, turn(z, -step[d]), half]
        return remote(piece, piece, ag_ss.at[k, j], ag_rs.at[k, j], in_plane(t, step[d]))

    def ag2f(j, t, d):
        k = t * 8 + 4 + d
        piece = hid.at[j, 0, :, z] if t == 0 else hid.at[j, 1, x]
        return remote(piece, piece, ag_ss.at[k, j], ag_rs.at[k, j], in_plane(1 - t, step[d]))

    def ag2h(j, t, d):
        k = t * 8 + 6 + d
        half = pl.ds(32 * d, 32)
        piece = hid.at[j, 0, :, turn(z, -step[d]), half] if t == 0 else hid.at[j, 1, turn(x, -step[d]), :, half]
        return remote(piece, piece, ag_ss.at[k, j], ag_rs.at[k, j], in_plane(1 - t, step[d]))

    copies = (rs1h, rs1f, rs2h, rs2f, ag1f, ag1h, ag2f, ag2h)
    weights = (w_gate, w_up)

    def prune(w, j, mask, rows_of):
        for a in range(w.shape[1] // BLOCK):
            for b in range(w.shape[2] // BLOCK):
                keep = rows_of(a, b)
                keep = jnp.full((16, BLOCK), mask[keep[0], keep[1]].astype(F32), F32).astype(BF16)
                view = (j, pl.ds(a * BLOCK, BLOCK), pl.ds(b * BLOCK, BLOCK))
                w[view] = (w[view].reshape(BLOCK // 16, 16, BLOCK) * keep[None]).reshape(BLOCK, BLOCK)

    def product(j, m, dest):
        lhs = tok[dest] if m == 0 else tok[:, dest]
        k = lhs.shape[-1]
        return jnp.dot(lhs.reshape(256, k), weights[m][j], preferred_element_type=F32).reshape(4, 64, cw)

    def stage_a(j):
        load_gate(j).wait()
        load_up(j).wait()
        prune(w_gate, j, gm, lambda a, b: (a, j * (cw // BLOCK) + b))
        prune(w_up, j, um, lambda a, b: (a, j * (cw // BLOCK) + b))
        for m in (0, 1):
            s1[j, m, 0] = product(j, m, turn(coord[m], 2)).astype(BF16)
            for d in (0, 1):
                rs1h(j, m, d).start()

    def stage_b(j):
        for m in (0, 1):
            for d in (0, 1):
                got = product(j, m, turn(coord[m], step[d]))
                rs1h(j, m, d).wait_recv()
                s1[j, m, 1 + d, pl.ds(2 * d, 2)] = (got[2 * d : 2 * d + 2] + r1h[j, m, d].astype(F32)).astype(BF16)
                s1[j, m, 1 + d, pl.ds(2 - 2 * d, 2)] = got[2 - 2 * d : 4 - 2 * d].astype(BF16)
                rs1f(j, m, d).start()

    def stage_c(j):
        slot = j % 4
        for m in (0, 1):
            got = product(j, m, coord[m])
            rs1f(j, m, 0).wait_recv()
            rs1f(j, m, 1).wait_recv()
            part[slot, m] = got + r1f[j, m, 0].astype(F32) + r1f[j, m, 1].astype(F32)
            s2[j, m, 0] = part[slot, m, turn(coord[1 - m], 2)].astype(BF16)
            for d in (0, 1):
                rs2h(j, m, d).start()

    def stage_d(j):
        slot = j % 4
        for m in (0, 1):
            for d in (0, 1):
                rs2h(j, m, d).wait_recv()
                got = part[slot, m, turn(coord[1 - m], step[d])]
                lo, hi = 32 * d, 32 - 32 * d
                s2[j, m, 1 + d, pl.ds(lo, 32)] = (got[lo : lo + 32] + r2h[j, m, d].astype(F32)).astype(BF16)
                s2[j, m, 1 + d, pl.ds(hi, 32)] = got[hi : hi + 32].astype(BF16)
                rs2f(j, m, d).start()

    def stage_e(j):
        slot = j % 4
        for m in (0, 1):
            for d in (0, 1):
                rs2f(j, m, d).wait_recv()
        g = part[slot, 0, z] + r2f[j, 0, 0].astype(F32) + r2f[j, 0, 1].astype(F32)
        u = part[slot, 1, x] + r2f[j, 1, 0].astype(F32) + r2f[j, 1, 1].astype(F32)
        h = (g / (1.0 + jnp.exp(-g)) * u).astype(BF16)
        hid[j, 0, x, z] = h[:, :half_cw]
        hid[j, 1, x, z] = h[:, half_cw:]
        for t in (0, 1):
            for d in (0, 1):
                ag1f(j, t, d).start()

    def relay(first, then):
        def stage(j):
            for t in (0, 1):
                for d in (0, 1):
                    first(j, t, d).wait_recv()
                    then(j, t, d).start()
        return stage

    def stage_g(j):
        for t in (0, 1):
            for d in (0, 1):
                ag1h(j, t, d).wait_recv()
            for d in (0, 1):
                ag2f(j, t, d).start()

    def stage_i(j):
        load_down(j).wait()
        prune(w_down, j, dm, lambda a, b: (j * (cw // BLOCK) + a, b))
        for t in (0, 1):
            for d in (0, 1):
                ag2h(j, t, d).wait_recv()
        for q in range(4):
            lhs = jnp.concatenate([hid[j, 0, q].reshape(256, half_cw), hid[j, 1, q].reshape(256, half_cw)], axis=1)
            got = jnp.dot(lhs, w_down[j], preferred_element_type=F32).reshape(2, 128, acc.shape[-1])
            acc[pl.ds(2 * q, 2)] = acc[pl.ds(2 * q, 2)] + got

    acc[...] = jnp.zeros_like(acc)
    stages = (stage_a, stage_b, stage_c, stage_d, stage_e, relay(ag1f, ag1h), stage_g, relay(ag2f, ag2h), stage_i)

    @pl.loop(0, ROUNDS + LAGS)
    def _(i):
        for lag, stage in enumerate(stages):
            @pl.when((i >= lag) & (i < ROUNDS + lag))
            def _(stage=stage, lag=lag):
                stage(i - lag)

    def o_twin(k):
        return remote(o_send.at[k], o_recv.at[k], out_ss.at[k], out_rs.at[k], twin)

    def oyh(d):
        return remote(oy_send.at[0, pl.ds(64 * d, 64)], oy_h.at[d], out_ss.at[4 + d], out_rs.at[4 + d], in_line(step[d]))

    def oyf(d):
        return remote(oy_send.at[1 + d], oy_f.at[d], out_ss.at[6 + d], out_rs.at[6 + d], in_line(step[d]))

    order = (2, 1, 3, 0)
    for k in order:
        o_send[k] = acc[turn(y, k) * 2 + 1 - core].astype(BF16)
        o_twin(k).start()

    def paired(k):
        o_twin(k).wait_recv()
        return acc[turn(y, k) * 2 + core] + o_recv[k].astype(F32)

    oy_send[0] = paired(2).astype(BF16)
    oyh(0).start()
    oyh(1).start()
    for d in (0, 1):
        got = paired(1 if d == 0 else 3)
        oyh(d).wait_recv()
        lo, hi = 64 * d, 64 - 64 * d
        oy_send[1 + d, pl.ds(lo, 64)] = (got[lo : lo + 64] + oy_h[d].astype(F32)).astype(BF16)
        oy_send[1 + d, pl.ds(hi, 64)] = got[hi : hi + 64].astype(BF16)
        oyf(d).start()
    got = paired(0)
    oyf(0).wait_recv()
    oyf(1).wait_recv()
    out_ref[...] = (got + oy_f[0].astype(F32) + oy_f[1].astype(F32)).astype(BF16)

    for d in (0, 1):
        tok_full(d).wait_send()
        tok_half(d).wait_send()
        oyh(d).wait_send()
        oyf(d).wait_send()
    for k in range(4):
        tok_twin(k).wait_send()
        o_twin(k).wait_send()

    @pl.loop(0, ROUNDS)
    def _(j):
        for copy in copies:
            for m in (0, 1):
                for d in (0, 1):
                    copy(j, m, d).wait_send()


def per_device(tokens, gate_weight, up_weight, down_weight, gate_mask, up_mask, down_mask):
    own, k = tokens.shape
    ff = gate_weight.shape[1]
    n = down_weight.shape[1]
    cw = ff // ROUNDS
    vmem, dma = pltpu.VMEM, pltpu.SemaphoreType.DMA
    anywhere = pl.BlockSpec(memory_space=pl.ANY)
    scalars = pl.BlockSpec(memory_space=pltpu.SMEM)
    return pl.pallas_call(
        layer_kernel,
        out_shape=jax.ShapeDtypeStruct((own, n), BF16),
        in_specs=[anywhere] * 4 + [scalars] * 3,
        out_specs=pl.BlockSpec(memory_space=pltpu.VMEM),
        scratch_shapes=[
            vmem((4, 4, 64, k), BF16),
            vmem((ROUNDS, k, cw), BF16),
            vmem((ROUNDS, k, cw), BF16),
            vmem((ROUNDS, cw, n), BF16),
            vmem((ROUNDS, 2, 3, 4, 64, cw), BF16),
            vmem((ROUNDS, 2, 2, 2, 64, cw), BF16),
            vmem((ROUNDS, 2, 2, 4, 64, cw), BF16),
            vmem((4, 2, 4, 64, cw), F32),
            vmem((ROUNDS, 2, 3, 64, cw), BF16),
            vmem((ROUNDS, 2, 2, 32, cw), BF16),
            vmem((ROUNDS, 2, 2, 64, cw), BF16),
            vmem((ROUNDS, 2, 4, 4, 64, cw // 2), BF16),
            vmem((8, own, n), F32),
            vmem((4, own, n), BF16),
            vmem((4, own, n), BF16),
            vmem((3, own, n), BF16),
            vmem((2, own // 2, n), BF16),
            vmem((2, own, n), BF16),
            dma((4, ROUNDS)),
            dma((8,)),
            dma((8,)),
            dma((16, ROUNDS)),
            dma((16, ROUNDS)),
            dma((16, ROUNDS)),
            dma((16, ROUNDS)),
            dma((8,)),
            dma((8,)),
        ],
        compiler_params=pltpu.CompilerParams(
            collective_id=0, has_side_effects=True, vmem_limit_bytes=67_043_328
        ),
    )(tokens.reshape(2, own // 2, k), gate_weight, up_weight, down_weight, gate_mask, up_mask, down_mask)


def solution(mesh):
    return jax.shard_map(
        per_device,
        mesh=mesh,
        in_specs=(
            P("row", "col"),
            P("col", "row"),
            P("col", "row"),
            P("row", "col"),
            P("col", "row"),
            P("col", "row"),
            P("row", "col"),
        ),
        out_specs=P("row", "col"),
        check_vma=False,
    )
```

time: 304 us -> 160 us (0.53)
  waiting for transfers between devices: 246 us -> 0 us
  Pallas kernels: 0 us -> 156 us
  matrix products: 25.1 us -> 0 us
  local copies, waits for them, and re-layouts: 18.9 us -> 2.94 us
  between operations: 13.1 us -> 0.01 us
    psum x1 -> x0, waiting for transfers between devices: 198 us -> none  [per_device(): lax.psum(up_part.astype(jnp.bfloat16), 'col').astype(jnp.float32)]
    pallas_call x0 -> x1, Pallas kernels: none -> 156 us  [per_device(): pl.pallas_call(layer_kernel, out_shape=jax.ShapeDtypeStruct((own, n), BF1...]
    reduce_scatter x1 -> x0, waiting for transfers between devices: 32.1 us -> none  [per_device(): lax.psum_scatter(jnp.dot(hidden, kept_down, preferred_element_type=jnp.fl...]
    dot_general x3 -> x0, matrix products: 25.1 us -> none  [the longest x1 11.6 us: per_device(): jnp.dot(hidden, kept_down, preferred_element_type=jnp.float32)]
    all_gather x1 -> x0, waiting for transfers between devices: 14.7 us -> none  [per_device(): gathered = lax.all_gather(tokens, 'row', axis=0, tiled=True)]
    unnamed x14 -> x2, local copies, waits for them, and re-layouts: 15.6 us -> 2.94 us
  transfers between devices with their start and end apart: 3 -> 0, of which waited for: 3 -> 0; matrix products, arithmetic and copies ran while one was open for 4% -> 0% of each run, Pallas kernels for 0% -> 0%
where the time goes in v1:
time: 160 us; the launch traced here: 159 us
  Pallas kernels  156 us (98%)
  local copies, waits for them, and re-layouts  2.94 us (2%)
    pallas_call x1, Pallas kernels, per_device(): pl.pallas_call(layer_kernel, out_shape=jax.ShapeDtypeStruct((own, n), BF1...  156 us

profile of v1, /device:TPU:0, one launch (start us, length us, event | category | flops | bytes accessed | tf_op | source)
XLA Modules:
  0.0 158.8 jit_solution(11195087518372583821)
XLA Ops:
  0.0 1.4 copy.8.dm
  1.4 155.9 %shard_map.73 = bf16[128,512]{1,0:T(8,128)(2,1)} custom-call(bf16[2,64,512]{2,1,0:T(8,128)(2,1)} %bitcast.1, bf16[512,3584]{1,0:T(8,128)(2,1)} %gate_hbm.1, bf16[512,3584]{1,0:T(8,128)(2,1)} %up_hbm.1, bf16[3584,512]{1,0:T(8,128)(2,1)} %down_hbm.1, s32[4,28]{1,0:T(4,128)} %gm.1, s32[4,28]{1,0:T(4,128)} %um.1, s32[28,4]{1,0:T(8,128)} %copy.8.dm), custom_call_target="tpu_custom_call" | custom-call | tf_op jit(solution)/shard_map/pallas_call | solution.py:305
  157.2 1.6 copy.10

commit v2 on v0

v2 whole, which is shorter than its diff:
```python
import jax
import jax.numpy as jnp
from jax import lax
from jax.experimental import pallas as pl
from jax.experimental.pallas import tpu as pltpu
from jax.sharding import PartitionSpec as P

BLOCK = 128
ROUNDS = 7
F32, BF16 = jnp.float32, jnp.bfloat16
MESH = pl.DeviceIdType.MESH
STEP = (1, -1)


def layer_kernel(
    tok_hbm, gate_hbm, up_hbm, down_hbm, gm, um, dm, out_ref,
    tok, w_own, w_out, w_in, w_down,
    s1, r1, part, s2, r2h, r2f, hid, acc, o_send, o_recv, oy_send, oy_h, oy_f,
    load_sem, down_sem, tok_load, tok_ss, tok_rs, twin_ss, twin_rs, w_ss, w_rs, rs_ss, rs_rs, ag_ss, ag_rs,
    out_ss, out_rs,
):
    row, col = lax.axis_index("row"), lax.axis_index("col")
    y, core = row // 2, row % 2
    x, z = col // 4, col % 4
    coord = (x, z)
    half = tuple(v // 2 for v in coord)
    kind = tuple(((v + 1) // 2) % 2 for v in coord)
    n = acc.shape[-1]

    def turn(v, k):
        return (v + k + 4) % 4

    def at(axis, v):
        return (row, v * 4 + z) if axis == 0 else (row, x * 4 + v)

    def in_plane(axis, k):
        return at(axis, turn(coord[axis], k))

    def odd(axis):
        return at(axis, coord[axis] + 1 - 2 * (coord[axis] % 2))

    def even(axis):
        return at(axis, 3 - coord[axis])

    def in_line(k):
        return (turn(y, k) * 2 + core, col)

    twin = (row + 1 - 2 * core, col)

    def remote(src, dst, ss, rs, device):
        return pltpu.make_async_remote_copy(
            src_ref=src, dst_ref=dst, send_sem=ss, recv_sem=rs, device_id=device, device_id_type=MESH
        )

    def block_of(t, c, j):
        return (2 * t + c) * ROUNDS + j

    def load_w(j, t, out, m):
        c = (1 - kind[t]) if out else kind[t]
        src = (up_hbm if m else gate_hbm).at[:, pl.ds(pl.multiple_of(block_of(t, c, j) * BLOCK, BLOCK), BLOCK)]
        dst = (w_out if out else w_own).at[j, t, :, pl.ds(m * BLOCK, BLOCK)]
        return pltpu.make_async_copy(src, dst, load_sem.at[t * 4 + out * 2 + m, j])

    def load_down(j, t, c):
        src = down_hbm.at[pl.ds(pl.multiple_of(block_of(t, c, j) * BLOCK, BLOCK), BLOCK)]
        return pltpu.make_async_copy(src, w_down.at[j, pl.ds((2 * t + c) * BLOCK, BLOCK)], down_sem.at[2 * t + c, j])

    load_tok = pltpu.make_async_copy(tok_hbm, tok.at[0, y, core], tok_load.at[0])
    load_tok.start()

    @pl.loop(0, ROUNDS)
    def _(j):
        for out in (1, 0):
            for t in (0, 1):
                for m in (0, 1):
                    load_w(j, t, out, m).start()

    @pl.loop(0, ROUNDS)
    def _(j):
        for t in (0, 1):
            for c in (0, 1):
                load_down(j, t, c).start()

    barrier = pltpu.get_barrier_semaphore()
    peers = [in_plane(a, k) for a in (0, 1) for k in STEP] + [in_line(k) for k in STEP] + [twin]
    for peer in peers:
        pl.semaphore_signal(barrier, inc=1, device_id=peer, device_id_type=MESH)
    pl.semaphore_wait(barrier, len(peers))

    def y_full(s, d):
        piece = tok.at[s, y, core]
        return remote(tok_hbm if s == 0 else piece, piece, tok_ss.at[2 * s + d], tok_rs.at[2 * s + d], in_line(STEP[d]))

    def y_half(d):
        piece = tok.at[0, turn(y, -STEP[d]), core, pl.ds(64 * d, 64)]
        return remote(piece, piece, tok_ss.at[6 + d], tok_rs.at[6 + d], in_line(STEP[d]))

    def odd_near(t):
        return remote(tok_hbm, tok.at[1 + t, y, core], tok_ss.at[8 + t], tok_rs.at[8 + t], odd(t))

    def odd_far(t):
        v = turn(y, 2)
        return remote(tok.at[0, v, core], tok.at[1 + t, v, core], tok_ss.at[10 + t], tok_rs.at[10 + t], odd(t))

    def to_twin(s, k):
        piece = tok.at[s, turn(y, k), core]
        return remote(piece, piece, twin_ss.at[s, k % 4], twin_rs.at[s, k % 4], twin)

    def send_w(j, t):
        return remote(w_out.at[j, t], w_in.at[j, t], w_ss.at[t, j], w_rs.at[t, j], odd(t))

    def prune(w, view, keep):
        keep = jnp.full((16, BLOCK), keep.astype(F32), F32).astype(BF16)
        w[view] = (w[view].reshape(BLOCK // 16, 16, BLOCK) * keep[None]).reshape(BLOCK, BLOCK)

    def stage_w(j):
        for out in (1, 0):
            w = w_out if out else w_own
            for t in (0, 1):
                c = (1 - kind[t]) if out else kind[t]
                for m in (0, 1):
                    load_w(j, t, out, m).wait()
                    for a in range(w.shape[2] // BLOCK):
                        view = (j, t, pl.ds(a * BLOCK, BLOCK), pl.ds(m * BLOCK, BLOCK))
                        prune(w, view, (um if m else gm)[a, block_of(t, c, j)])
                if out:
                    send_w(j, t).start()

    def rs1(j, t):
        return remote(s1.at[j, t], r1.at[j, t], rs_ss.at[t * 5, j], rs_rs.at[t * 5, j], even(t))

    def rs2h(j, t, d):
        k = t * 5 + 1 + d
        return remote(s2.at[j, t, 0, pl.ds(64 * d, 64)], r2h.at[j, t, d], rs_ss.at[k, j], rs_rs.at[k, j], in_plane(1 - t, STEP[d]))

    def rs2f(j, t, d):
        k = t * 5 + 3 + d
        return remote(s2.at[j, t, 1 + d], r2f.at[j, t, d], rs_ss.at[k, j], rs_rs.at[k, j], in_plane(1 - t, STEP[d]))

    def ag1f(j, t, d):
        k = t * 8 + d
        piece = hid.at[j, t, x, z]
        return remote(piece, piece, ag_ss.at[k, j], ag_rs.at[k, j], in_plane(t, STEP[d]))

    def ag1h(j, t, d):
        k = t * 8 + 2 + d
        rows = pl.ds(64 * d, 64)
        piece = hid.at[j, 0, turn(x, -STEP[d]), z, rows] if t == 0 else hid.at[j, 1, x, turn(z, -STEP[d]), rows]
        return remote(piece, piece, ag_ss.at[k, j], ag_rs.at[k, j], in_plane(t, STEP[d]))

    def ag2f(j, t, d):
        k = t * 8 + 4 + d
        piece = hid.at[j, 0, :, z] if t == 0 else hid.at[j, 1, x]
        return remote(piece, piece, ag_ss.at[k, j], ag_rs.at[k, j], in_plane(1 - t, STEP[d]))

    def ag2h(j, t, d):
        k = t * 8 + 6 + d
        rows = pl.ds(64 * d, 64)
        piece = hid.at[j, 0, :, turn(z, -STEP[d]), rows] if t == 0 else hid.at[j, 1, turn(x, -STEP[d]), :, rows]
        return remote(piece, piece, ag_ss.at[k, j], ag_rs.at[k, j], in_plane(1 - t, STEP[d]))

    def product(j, t, h):
        rows, k = pl.ds(2 * h, 2), tok.shape[-1]
        got = jnp.dot(tok[0, rows].reshape(512, k), w_own[j, t], preferred_element_type=F32)
        got = got + jnp.dot(tok[1 + t, rows].reshape(512, k), w_in[j, t], preferred_element_type=F32)
        return got.reshape(4, 128, 2 * BLOCK)

    def stage_a(j):
        for t in (0, 1):
            send_w(j, t).wait_recv()
            s1[j, t] = product(j, t, 1 - half[t]).astype(BF16)
            rs1(j, t).start()

    def stage_b(j):
        for t in (0, 1):
            got = product(j, t, half[t])
            rs1(j, t).wait_recv()
            part[j % 4, t] = got + r1[j, t].astype(F32)
            s2[j, t, 0] = part[j % 4, t, turn(coord[1 - t], 2)].astype(BF16)
            for d in (0, 1):
                rs2h(j, t, d).start()

    def stage_c(j):
        for t in (0, 1):
            for d in (0, 1):
                rs2h(j, t, d).wait_recv()
                got = part[j % 4, t, turn(coord[1 - t], STEP[d])]
                lo, hi = 64 * d, 64 - 64 * d
                s2[j, t, 1 + d, pl.ds(lo, 64)] = (got[lo : lo + 64] + r2h[j, t, d].astype(F32)).astype(BF16)
                s2[j, t, 1 + d, pl.ds(hi, 64)] = got[hi : hi + 64].astype(BF16)
                rs2f(j, t, d).start()

    def stage_d(j):
        for t in (0, 1):
            for d in (0, 1):
                rs2f(j, t, d).wait_recv()
            got = part[j % 4, t, coord[1 - t]] + r2f[j, t, 0].astype(F32) + r2f[j, t, 1].astype(F32)
            g, u = got[:, :BLOCK], got[:, BLOCK:]
            hid[j, t, x, z] = (g / (1.0 + jnp.exp(-g)) * u).astype(BF16)
            for d in (0, 1):
                ag1f(j, t, d).start()

    def relay(first, then):
        def stage(j):
            for t in (0, 1):
                for d in (0, 1):
                    first(j, t, d).wait_recv()
                    then(j, t, d).start()
        return stage

    def stage_f(j):
        for t in (0, 1):
            for d in (0, 1):
                ag1h(j, t, d).wait_recv()
            for d in (0, 1):
                ag2f(j, t, d).start()

    def stage_h(j):
        for t in (0, 1):
            for c in (0, 1):
                load_down(j, t, c).wait()
                for b in range(n // BLOCK):
                    prune(w_down, (j, pl.ds((2 * t + c) * BLOCK, BLOCK), pl.ds(b * BLOCK, BLOCK)), dm[b, block_of(t, c, j)])
        for t in (0, 1):
            for d in (0, 1):
                ag2h(j, t, d).wait_recv()
        for h, (first, second) in enumerate(((0, 1), (3, 2))):
            lhs = [hid[j, 0, first], hid[j, 0, second], hid[j, 1, :, first], hid[j, 1, :, second]]
            lhs = jnp.concatenate([v.reshape(512, BLOCK) for v in lhs], axis=1)
            got = jnp.dot(lhs, w_down[j], preferred_element_type=F32).reshape(4, 128, n)
            acc[pl.ds(4 * h, 4)] = acc[pl.ds(4 * h, 4)] + got

    for d in (0, 1):
        y_full(0, d).start()
    for t in (0, 1):
        odd_near(t).start()
    load_tok.wait()
    to_twin(0, 0).start()
    acc[...] = jnp.zeros_like(acc)
    stage_w(0)
    for d in (0, 1):
        y_full(0, d).wait_recv()
        y_half(d).start()
        to_twin(0, -STEP[d]).start()
    for t in (0, 1):
        odd_near(t).wait_recv()
        for d in (0, 1):
            y_full(1 + t, d).start()
        to_twin(1 + t, 0).start()
    for d in (0, 1):
        y_half(d).wait_recv()
    for t in (0, 1):
        odd_far(t).start()
    to_twin(0, 2).start()
    stage_w(1)
    for t in (0, 1):
        for d in (0, 1):
            y_full(1 + t, d).wait_recv()
            to_twin(1 + t, -STEP[d]).start()
    for t in (0, 1):
        odd_far(t).wait_recv()
        to_twin(1 + t, 2).start()
    for s in range(3):
        for k in range(4):
            to_twin(s, k).wait_recv()

    stages = (
        (stage_w, -2),
        (stage_a, 0),
        (stage_b, 1),
        (stage_c, 2),
        (stage_d, 3),
        (relay(ag1f, ag1h), 4),
        (stage_f, 5),
        (relay(ag2f, ag2h), 6),
        (stage_h, 7),
    )

    @pl.loop(0, ROUNDS + 7)
    def _(i):
        for stage, lag in stages:
            @pl.when((i >= lag) & (i < ROUNDS + lag))
            def _(stage=stage, lag=lag):
                stage(i - lag)

    def o_twin(k):
        return remote(o_send.at[k], o_recv.at[k], out_ss.at[k], out_rs.at[k], twin)

    def oyh(d):
        return remote(oy_send.at[0, pl.ds(64 * d, 64)], oy_h.at[d], out_ss.at[4 + d], out_rs.at[4 + d], in_line(STEP[d]))

    def oyf(d):
        return remote(oy_send.at[1 + d], oy_f.at[d], out_ss.at[6 + d], out_rs.at[6 + d], in_line(STEP[d]))

    for k in (2, 1, 3, 0):
        o_send[k] = acc[turn(y, k) * 2 + 1 - core].astype(BF16)
        o_twin(k).start()

    def paired(k):
        o_twin(k).wait_recv()
        return acc[turn(y, k) * 2 + core] + o_recv[k].astype(F32)

    oy_send[0] = paired(2).astype(BF16)
    for d in (0, 1):
        oyh(d).start()
    for d in (0, 1):
        got = paired(1 if d == 0 else 3)
        oyh(d).wait_recv()
        lo, hi = 64 * d, 64 - 64 * d
        oy_send[1 + d, pl.ds(lo, 64)] = (got[lo : lo + 64] + oy_h[d].astype(F32)).astype(BF16)
        oy_send[1 + d, pl.ds(hi, 64)] = got[hi : hi + 64].astype(BF16)
        oyf(d).start()
    got = paired(0)
    for d in (0, 1):
        oyf(d).wait_recv()
    out_ref[...] = (got + oy_f[0].astype(F32) + oy_f[1].astype(F32)).astype(BF16)

    for d in (0, 1):
        for s in range(3):
            y_full(s, d).wait_send()
        y_half(d).wait_send()
        odd_near(d).wait_send()
        odd_far(d).wait_send()
        oyh(d).wait_send()
        oyf(d).wait_send()
    for k in range(4):
        for s in range(3):
            to_twin(s, k).wait_send()
        o_twin(k).wait_send()

    @pl.loop(0, ROUNDS)
    def _(j):
        for t in (0, 1):
            send_w(j, t).wait_send()
            rs1(j, t).wait_send()
            for d in (0, 1):
                for copy in (rs2h, rs2f, ag1f, ag1h, ag2f, ag2h):
                    copy(j, t, d).wait_send()


def per_device(tokens, gate_weight, up_weight, down_weight, gate_mask, up_mask, down_mask):
    own, k = tokens.shape
    n = down_weight.shape[1]
    vmem, dma = pltpu.VMEM, pltpu.SemaphoreType.DMA
    anywhere = pl.BlockSpec(memory_space=pl.ANY)
    scalars = pl.BlockSpec(memory_space=pltpu.SMEM)
    return pl.pallas_call(
        layer_kernel,
        out_shape=jax.ShapeDtypeStruct((own, n), BF16),
        in_specs=[anywhere] * 4 + [scalars] * 3,
        out_specs=pl.BlockSpec(memory_space=pltpu.VMEM),
        scratch_shapes=[
            vmem((3, 4, 2, own, k), BF16),
            vmem((ROUNDS, 2, k, 2 * BLOCK), BF16),
            vmem((ROUNDS, 2, k, 2 * BLOCK), BF16),
            vmem((ROUNDS, 2, k, 2 * BLOCK), BF16),
            vmem((ROUNDS, 4 * BLOCK, n), BF16),
            vmem((ROUNDS, 2, 4, own, 2 * BLOCK), BF16),
            vmem((ROUNDS, 2, 4, own, 2 * BLOCK), BF16),
            vmem((4, 2, 4, own, 2 * BLOCK), F32),
            vmem((ROUNDS, 2, 3, own, 2 * BLOCK), BF16),
            vmem((ROUNDS, 2, 2, own // 2, 2 * BLOCK), BF16),
            vmem((ROUNDS, 2, 2, own, 2 * BLOCK), BF16),
            vmem((ROUNDS, 2, 4, 4, own, BLOCK), BF16),
            vmem((8, own, n), F32),
            vmem((4, own, n), BF16),
            vmem((4, own, n), BF16),
            vmem((3, own, n), BF16),
            vmem((2, own // 2, n), BF16),
            vmem((2, own, n), BF16),
            dma((8, ROUNDS)),
            dma((4, ROUNDS)),
            dma((1,)),
            dma((12,)),
            dma((12,)),
            dma((3, 4)),
            dma((3, 4)),
            dma((2, ROUNDS)),
            dma((2, ROUNDS)),
            dma((10, ROUNDS)),
            dma((10, ROUNDS)),
            dma((16, ROUNDS)),
            dma((16, ROUNDS)),
            dma((8,)),
            dma((8,)),
        ],
        compiler_params=pltpu.CompilerParams(
            collective_id=0, has_side_effects=True, vmem_limit_bytes=67_043_328
        ),
    )(tokens, gate_weight, up_weight, down_weight, gate_mask, up_mask, down_mask.T)


def solution(mesh):
    return jax.shard_map(
        per_device,
        mesh=mesh,
        in_specs=(
            P("row", "col"),
            P("col", "row"),
            P("col", "row"),
            P("row", "col"),
            P("col", "row"),
            P("col", "row"),
            P("row", "col"),
        ),
        out_specs=P("row", "col"),
        check_vma=False,
    )
```

time: 304 us -> 136 us (0.45)
  waiting for transfers between devices: 246 us -> 0 us
  Pallas kernels: 0 us -> 134 us
  matrix products: 25.1 us -> 0 us
  local copies, waits for them, and re-layouts: 18.9 us -> 1.57 us
  between operations: 13.1 us -> 0.01 us
    psum x1 -> x0, waiting for transfers between devices: 198 us -> none  [per_device(): lax.psum(up_part.astype(jnp.bfloat16), 'col').astype(jnp.float32)]
    pallas_call x0 -> x1, Pallas kernels: none -> 134 us  [per_device(): pl.pallas_call(layer_kernel, out_shape=jax.ShapeDtypeStruct((own, n), BF1...]
    reduce_scatter x1 -> x0, waiting for transfers between devices: 32.1 us -> none  [per_device(): lax.psum_scatter(jnp.dot(hidden, kept_down, preferred_element_type=jnp.fl...]
    dot_general x3 -> x0, matrix products: 25.1 us -> none  [the longest x1 11.6 us: per_device(): jnp.dot(hidden, kept_down, preferred_element_type=jnp.float32)]
    all_gather x1 -> x0, waiting for transfers between devices: 14.7 us -> none  [per_device(): gathered = lax.all_gather(tokens, 'row', axis=0, tiled=True)]
    unnamed x14 -> x1, local copies, waits for them, and re-layouts: 15.6 us -> 1.57 us
  transfers between devices with their start and end apart: 3 -> 0, of which waited for: 3 -> 0; matrix products, arithmetic and copies ran while one was open for 4% -> 0% of each run, Pallas kernels for 0% -> 0%
where the time goes in v2:
time: 136 us
  Pallas kernels  134 us (99%)
  local copies, waits for them, and re-layouts  1.57 us (1%)
    pallas_call x1, Pallas kernels, per_device(): pl.pallas_call(layer_kernel, out_shape=jax.ShapeDtypeStruct((own, n), BF1...  134 us

profile of v2, /device:TPU:0, one launch (start us, length us, event | category | flops | bytes accessed | tf_op | source)
XLA Modules:
  0.0 135.7 jit_solution(17073949176328080492)
XLA Ops:
  0.0 134.2 %shard_map.73 = bf16[128,512]{1,0:T(8,128)(2,1)} custom-call(bf16[128,512]{1,0:T(8,128)(2,1)} %tok_hbm.1, bf16[512,3584]{1,0:T(8,128)(2,1)} %gate_hbm.1, bf16[512,3584]{1,0:T(8,128)(2,1)} %up_hbm.1, bf16[3584,512]{1,0:T(8,128)(2,1)} %down_hbm.1, s32[4,28]{1,0:T(4,128)} %gm.1, s32[4,28]{1,0:T(4,128)} %um.1, s32[4,28]{1,0:T(4,128)} %bitcast.1), custom_call_target="tpu_custom_call" | custom-call | tf_op jit(solution)/shard_map/pallas_call | solution.py:347
  134.2 1.6 %copy.9 = bf16[128,512]{1,0:T(8,128)(2,1)} copy(bf16[128,512]{1,0:T(8,128)(2,1)} %shard_map.73) | data formatting | bytes 262144

commit v3 on v2

--- a/solution.py
+++ b/solution.py
@@ -215,7 +215,7 @@
             for d in (0, 1):
                 ag2f(j, t, d).start()
 
-    def stage_h(j):
+    def ready(j):
         for t in (0, 1):
             for c in (0, 1):
                 load_down(j, t, c).wait()
@@ -224,6 +224,9 @@
         for t in (0, 1):
             for d in (0, 1):
                 ag2h(j, t, d).wait_recv()
+
+    def stage_h(j):
+        ready(j)
         for h, (first, second) in enumerate(((0, 1), (3, 2))):
             lhs = [hid[j, 0, first], hid[j, 0, second], hid[j, 1, :, first], hid[j, 1, :, second]]
             lhs = jnp.concatenate([v.reshape(512, BLOCK) for v in lhs], axis=1)
@@ -276,7 +279,7 @@
         (stage_h, 7),
     )
 
-    @pl.loop(0, ROUNDS + 7)
+    @pl.loop(0, ROUNDS + 6)
     def _(i):
         for stage, lag in stages:
             @pl.when((i >= lag) & (i < ROUNDS + lag))
@@ -292,17 +295,28 @@
     def oyf(d):
         return remote(oy_send.at[1 + d], oy_f.at[d], out_ss.at[6 + d], out_rs.at[6 + d], in_line(STEP[d]))
 
-    for k in (2, 1, 3, 0):
-        o_send[k] = acc[turn(y, k) * 2 + 1 - core].astype(BF16)
+    def last_product(k):
+        j, v = ROUNDS - 1, turn(y, k)
+        h, pair = v // 2, pl.ds(2 * (v % 2), 2)
+        lhs = [hid[j, 0, 3 * h, pair], hid[j, 0, 1 + h, pair], hid[j, 1, pair, 3 * h], hid[j, 1, pair, 1 + h]]
+        lhs = jnp.concatenate([p.reshape(256, BLOCK) for p in lhs], axis=1)
+        got = jnp.dot(lhs, w_down[j], preferred_element_type=F32).reshape(2, 128, n)
+        acc[pl.ds(2 * v, 2)] = acc[pl.ds(2 * v, 2)] + got
+        o_send[k] = acc[2 * v + 1 - core].astype(BF16)
         o_twin(k).start()
 
     def paired(k):
         o_twin(k).wait_recv()
         return acc[turn(y, k) * 2 + core] + o_recv[k].astype(F32)
 
+    ready(ROUNDS - 1)
+    for k in (2, 1):
+        last_product(k)
     oy_send[0] = paired(2).astype(BF16)
     for d in (0, 1):
         oyh(d).start()
+    for k in (3, 0):
+        last_product(k)
     for d in (0, 1):
         got = paired(1 if d == 0 else 3)
         oyh(d).wait_recv()

time: 136 us -> 135 us (level)
  no operation moved by 1% of the time
where the time goes in v3:
time: 135 us
  Pallas kernels  134 us (99%)
  local copies, waits for them, and re-layouts  1.57 us (1%)
    pallas_call x1, Pallas kernels, per_device(): pl.pallas_call(layer_kernel, out_shape=jax.ShapeDtypeStruct((own, n), BF1...  134 us

profile of v3, /device:TPU:0, one launch (start us, length us, event | category | flops | bytes accessed | tf_op | source)
XLA Modules:
  0.0 135.3 jit_solution(9973817517609657496)
XLA Ops:
  0.0 133.8 %shard_map.73 = bf16[128,512]{1,0:T(8,128)(2,1)} custom-call(bf16[128,512]{1,0:T(8,128)(2,1)} %tok_hbm.1, bf16[512,3584]{1,0:T(8,128)(2,1)} %gate_hbm.1, bf16[512,3584]{1,0:T(8,128)(2,1)} %up_hbm.1, bf16[3584,512]{1,0:T(8,128)(2,1)} %down_hbm.1, s32[4,28]{1,0:T(4,128)} %gm.1, s32[4,28]{1,0:T(4,128)} %um.1, s32[4,28]{1,0:T(4,128)} %bitcast.1), custom_call_target="tpu_custom_call" | custom-call | tf_op jit(solution)/shard_map/pallas_call | solution.py:361
  133.8 1.6 %copy.9 = bf16[128,512]{1,0:T(8,128)(2,1)} copy(bf16[128,512]{1,0:T(8,128)(2,1)} %shard_map.73) | data formatting | bytes 262144
